TPU v7x, 32 devices: a whole 2x2x4 slice. The times are simulated.
32 devices in a mesh: groups: 2 (over x), seq: 16 (over z, y, core).
Axes of the slice: x: 2, y: 2, z: 4, core: 2. Of those that a mesh axis runs over, the one named last changes fastest.
Arguments:
- queries: bfloat16 [8192, 4096], P(('groups', 'seq')), parts along dimension 0, may hold values from -6 to 6
- key_rows: bfloat16 [8192, 2048], P(('groups', 'seq')), parts along dimension 0, may hold values from -6 to 6
- value_matrix: bfloat16 [8192, 2048], P(('groups', 'seq')), parts along dimension 0, may hold values from -6 to 6
Outputs:
- attended: bfloat16 [8192, 4096], P(('groups', 'seq')), parts along dimension 0
There are 2 independent parts, one for each index of `groups`. A program takes and returns all parts, laid end to end along the dimension named above; each array names one. Nothing has to cross between parts.
All inputs are finite; a program needn't handle non-finite values.
Results may differ from a plain program's by a relative error of at most 0.0045.
Values may be sent and summed in bfloat16 or wider, within the bound.
No kernel may reach another device: no remote copies, remote signals or barrier semaphores. Data moves between devices by JAX's collectives and lax.ppermute only.
A program may use at most 64 MiB of HBM per device.

v0:
```python
import functools

import jax
import jax.numpy as jnp
from jax import lax
from jax.experimental import pallas as pl
from jax.experimental.pallas import tpu as pltpu
from jax.sharding import PartitionSpec as P


QUERY_HEADS = 32
KEY_VALUE_HEADS = 16
HEAD_WIDTH = 128
WINDOW = 1024
GROUP = QUERY_HEADS // KEY_VALUE_HEADS

score_scale = 168.0 ** (-0.5)
LOG2_E = 1.4426950408889634
masked_value = -1e30
CHUNKS = (2, 2, 2, 2, 2, 2, 2, 2)
UNROLL = 2


def pack_kernel(key_ref, value_ref, out_ref):
    length = key_ref.shape[0]
    for head in range(out_ref.shape[0]):
        columns = slice(head * HEAD_WIDTH, (head + 1) * HEAD_WIDTH)
        out_ref[head, :length] = key_ref[:, columns]
        for start in range(0, length, HEAD_WIDTH):
            rows = slice(length + start, length + start + HEAD_WIDTH)
            out_ref[head, rows] = value_ref[start : start + HEAD_WIDTH, columns].T


def pack(key_rows, value_matrix, first, heads):
    length = key_rows.shape[0]
    spec = pl.BlockSpec((length, heads * HEAD_WIDTH), lambda _: (0, first // heads))
    if first == 0:
        key_rows = pltpu.with_memory_space_constraint(key_rows, pltpu.HBM)
        value_matrix = pltpu.with_memory_space_constraint(value_matrix, pltpu.HBM)
    return pl.pallas_call(
        pack_kernel,
        out_shape=jax.ShapeDtypeStruct((heads, 2 * length, HEAD_WIDTH), key_rows.dtype),
        grid=(1,),
        in_specs=[spec, spec],
        out_specs=pl.BlockSpec((heads, 2 * length, HEAD_WIDTH), lambda _: (0, 0, 0)),
        compiler_params=pltpu.CompilerParams(vmem_limit_bytes=8 << 20),
        cost_estimate=pl.CostEstimate(
            flops=0, transcendentals=0, bytes_accessed=8 * heads * length * HEAD_WIDTH
        ),
    )(key_rows, value_matrix)


def attend_kernel(parts, early, late, q_ref, *rest):
    rest = list(rest)
    own_ref, far_ref = (rest.pop(0), rest.pop(0)) if 0 in parts else (None, None)
    others = {part: rest.pop(0) for part in parts if part}
    if late:
        before_ref, before_max_ref = rest.pop(0), rest.pop(0)
    score_ref, max_ref = rest[-2:]
    if early:
        total_ref, total_max_ref = rest[-4:-2]
    else:
        o_ref = rest[-3]
    kv_ref = others[parts[-1]]
    heads, length = kv_ref.shape[0], q_ref.shape[0]
    block = lax.axis_index("seq")
    odd = lax.rem(block, 2)

    def bias_of(back):
        return jnp.where(block >= back, 0.0, masked_value).astype(jnp.float32)

    far_bias = bias_of(4)
    biases = (0.0, bias_of(2), bias_of(3 - 2 * odd), bias_of(1 + 2 * odd))
    across = (((1,), (1,)), ((), ()))
    scale = score_scale * LOG2_E
    ones = jnp.ones((16, length), jnp.bfloat16)
    key_pos = lax.broadcasted_iota(jnp.int32, (length, length), 0)
    query_pos = lax.broadcasted_iota(jnp.int32, (length, length), 1)
    causal = key_pos <= query_pos

    def columns(unit):
        return pl.ds(pl.multiple_of(unit * HEAD_WIDTH, HEAD_WIDTH), HEAD_WIDTH)

    def score(unit, part, row_max):
        head = lax.div(unit, GROUP)
        query = q_ref[:, columns(unit)]

        def product(ref):
            return lax.dot_general(
                ref[head, :length], query, across, preferred_element_type=jnp.float32
            )

        if part == 0:
            raw = jnp.where(causal, product(own_ref), product(far_ref) + far_bias)
        else:
            raw = product(others[part])
        slot = parts.index(part) * length
        score_ref[slot : slot + length] = raw
        largest = jnp.max(raw.reshape(length // 8, 8, length), axis=0) + biases[part]
        return largest if row_max is None else jnp.maximum(row_max, largest)

    def keep_max(unit, row_max):
        row_max = jnp.max(row_max, axis=0, keepdims=True) * scale
        row_max = jnp.broadcast_to(row_max, max_ref.shape)
        max_ref[...] = jnp.maximum(row_max, before_max_ref[unit]) if late else row_max

    def weigh(unit, part, total):
        head = lax.div(unit, GROUP)
        shift = max_ref[0:1] - biases[part] * scale
        slot = parts.index(part) * length
        weights = jnp.exp2(score_ref[slot : slot + length] * scale - shift)
        if part == 0:
            pieces = (
                (own_ref, jnp.where(causal, weights, 0.0)),
                (far_ref, jnp.where(causal, 0.0, weights)),
            )
        else:
            pieces = ((others[part], weights),)
        for ref, piece in pieces:
            values = jnp.concatenate(
                [
                    ref[head, length + start : length + start + HEAD_WIDTH]
                    for start in range(0, length, HEAD_WIDTH)
                ],
                axis=1,
            )
            product = jnp.dot(
                jnp.concatenate([values, ones], axis=0),
                piece.astype(jnp.bfloat16),
                preferred_element_type=jnp.float32,
            )
            total = product if total is None else total + product
        return total

    row_max = None
    for part in parts:
        row_max = score(0, part, row_max)
    keep_max(0, row_max)
    units = heads * GROUP

    def step(unit, _):
        row_max = total = None
        if late:
            total = before_ref[unit] * jnp.exp2(before_max_ref[unit, 0:1] - max_ref[0:1])
        if early:
            total_max_ref[unit] = max_ref[...]
        following = jnp.minimum(unit + 1, units - 1)
        for part in parts:
            total = weigh(unit, part, total)
            row_max = score(following, part, row_max)
        keep_max(following, row_max)
        if early:
            total_ref[unit] = total
        else:
            result = total[:HEAD_WIDTH] / total[HEAD_WIDTH : HEAD_WIDTH + 1]
            o_ref[:, columns(unit)] = result.T.astype(o_ref.dtype)
        return 0

    lax.fori_loop(0, units, step, 0, unroll=UNROLL if len(parts) == 4 else units)


def attend(queries, pieces, first, heads, output, parts=(0, 1, 2, 3), early=False, before=()):
    length = queries.shape[0]
    units = heads * GROUP
    sums = (units, HEAD_WIDTH + 16, length)
    maxima = (units, 8, length)

    def whole(shape):
        return pl.BlockSpec(shape, lambda _: (0,) * len(shape))

    q_spec = pl.BlockSpec((length, units * HEAD_WIDTH), lambda _: (0, first // heads))
    args = [queries, *pieces, *before]
    specs = [q_spec] + [whole(arg.shape) for arg in args[1:]]
    aliases = {}
    if output is not None:
        aliases = {len(args): 0}
        specs.append(pl.BlockSpec(memory_space=pl.ANY))
        args.append(output)
    out_shape = jax.ShapeDtypeStruct(queries.shape, queries.dtype)
    out_specs = q_spec
    if early:
        out_shape = tuple(jax.ShapeDtypeStruct(shape, jnp.float32) for shape in (sums, maxima))
        out_specs = tuple(whole(shape) for shape in (sums, maxima))
    keys = len(pieces) * length
    return pl.pallas_call(
        functools.partial(attend_kernel, parts, early, bool(before)),
        out_shape=out_shape,
        grid=(1,),
        in_specs=specs,
        out_specs=out_specs,
        scratch_shapes=[
            pltpu.VMEM((len(parts) * length, length), jnp.float32),
            pltpu.VMEM((8, length), jnp.float32),
        ],
        input_output_aliases=aliases,
        compiler_params=pltpu.CompilerParams(vmem_limit_bytes=16 << 20),
        cost_estimate=pl.CostEstimate(
            flops=units * length * keys * HEAD_WIDTH * 4,
            transcendentals=units * length * len(parts) * length,
            bytes_accessed=heads * HEAD_WIDTH * length * 2 * (2 * len(pieces) + 2 * GROUP),
        ),
    )(*args)


def per_device(queries, key_rows, value_matrix):
    length = queries.shape[0]
    devices = lax.axis_size("seq")
    assert WINDOW == 4 * length and devices % 4 == 0
    ring = [(i, (i + 4) % devices) for i in range(devices)]
    chain = ring[:-4]
    swap = [(i, i + 2 if i % 4 < 2 else i - 2) for i in range(devices)]
    pair = [(i, i ^ 1) for i in range(devices)]
    block = lax.axis_index("seq").astype(jnp.int32)
    upper = lax.rem(block, 4) >= 2
    odd = lax.rem(block, 2) == 1
    key_rows, value_matrix, upper, odd = lax.optimization_barrier(
        (key_rows, value_matrix, upper, odd)
    )

    bounds = [0]
    for heads in CHUNKS:
        bounds.append(bounds[-1] + heads)
    assert bounds[-1] == KEY_VALUE_HEADS
    own = []
    for first, heads in zip(bounds, CHUNKS):
        assert first % heads == 0
        own.append(pack(key_rows, value_matrix, first, heads))

    def send(piece, pairs):
        return lax.ppermute(piece, "seq", pairs)

    output = None
    for chunk, heads in enumerate(CHUNKS):
        mine = own[chunk]
        distant = send(mine, ring if chunk else chain)
        middle = send(jnp.where(upper, distant, mine), swap)
        pair1 = send(jnp.where(odd, distant, mine), pair)
        pair2 = send(middle, pair)
        first = bounds[chunk]
        pieces = (mine, distant, middle, pair1, pair2)
        options = {}
        if chunk == len(CHUNKS) - 1:
            before = attend(
                queries, (mine, distant, pair1), first, heads, None, parts=(0, 2), early=True
            )
            before = attend(
                queries, (middle,), first, heads, None, parts=(1,), early=True, before=before
            )
            pieces = (pair2,)
            options = {"parts": (3,), "before": before}
        output = attend(queries, pieces, first, heads, output, **options)
    return output


def solution(mesh):
    rows = P(("groups", "seq"), None)
    return jax.shard_map(
        per_device, mesh=mesh, in_specs=(rows, rows, rows), out_specs=rows, check_vma=False
    )
```

profile of v0, /device:TPU:26, one launch (start us, length us, event | category | flops | bytes accessed | tf_op | source)
XLA Modules:
  0.0 114.4 jit_solution(7775684744307449403)
XLA Ops:
  2.7 2.5 %collective-permute-start.24 = (bf16[2,512,128]{2,1,0:T(8,128)(2,1)S(1)}, bf16[2,512,128]{2,1,0:T(8,128)(2,1)S(1)}, u32[]{:S(2)}, u32[]{:S(2)}) collective-permute-start(bf16[2,512,128]{2,1,0:T(8,128)(2,1)S(1)} %shard_map.45.rest_0_), channel_id=1, source_target_pairs={{0,4},{1,5},{2,6},{3,7},{4,8},{5,9},{6,10},{7,11},{8,12},{9,13},{1... | collective-permute-start | bytes 786440 | tf_op jit(solution)/shard_map/ppermute | solution.py:230
  5.3 1.6 %collective-permute-start.20 = (bf16[2,512,128]{2,1,0:T(8,128)(2,1)S(1)}, bf16[2,512,128]{2,1,0:T(8,128)(2,1)S(1)}, u32[]{:S(2)}, u32[]{:S(2)}) collective-permute-start(bf16[2,512,128]{2,1,0:T(8,128)(2,1)S(1)} %shard_map.44.rest_0_), channel_id=1, source_target_pairs={{0,4},{1,5},{2,6},{3,7},{4,8},{5,9},{6,10},{7,11},{8,12},{9,13},{1... | collective-permute-start | bytes 786440 | tf_op jit(solution)/shard_map/ppermute | solution.py:230
  7.0 1.6 %collective-permute-start.16 = (bf16[2,512,128]{2,1,0:T(8,128)(2,1)S(1)}, bf16[2,512,128]{2,1,0:T(8,128)(2,1)S(1)}, u32[]{:S(2)}, u32[]{:S(2)}) collective-permute-start(bf16[2,512,128]{2,1,0:T(8,128)(2,1)S(1)} %shard_map.43.rest_0_), channel_id=1, source_target_pairs={{0,4},{1,5},{2,6},{3,7},{4,8},{5,9},{6,10},{7,11},{8,12},{9,13},{1... | collective-permute-start | bytes 786440 | tf_op jit(solution)/shard_map/ppermute | solution.py:230
  9.2 3.1 %collective-permute-done.28.rest_1_ = bf16[2,512,128]{2,1,0:T(8,128)(2,1)S(1)} collective-permute-done((bf16[2,512,128]{2,1,0:T(8,128)(2,1)S(1)}, bf16[2,512,128]{2,1,0:T(8,128)(2,1)S(1)}, u32[]{:S(2)}, u32[]{:S(2)}) %collective-permute-start.28) | collective-permute-done | bytes 262176 | tf_op jit(solution)/shard_map/ppermute | solution.py:230
  12.4 5.6 %collective-permute-done.24.rest_1_ = bf16[2,512,128]{2,1,0:T(8,128)(2,1)S(1)} collective-permute-done((bf16[2,512,128]{2,1,0:T(8,128)(2,1)S(1)}, bf16[2,512,128]{2,1,0:T(8,128)(2,1)S(1)}, u32[]{:S(2)}, u32[]{:S(2)}) %collective-permute-start.24) | collective-permute-done | bytes 262176 | tf_op jit(solution)/shard_map/ppermute | solution.py:230
  18.0 5.6 %collective-permute-done.20.rest_1_ = bf16[2,512,128]{2,1,0:T(8,128)(2,1)S(1)} collective-permute-done((bf16[2,512,128]{2,1,0:T(8,128)(2,1)S(1)}, bf16[2,512,128]{2,1,0:T(8,128)(2,1)S(1)}, u32[]{:S(2)}, u32[]{:S(2)}) %collective-permute-start.20) | collective-permute-done | bytes 262176 | tf_op jit(solution)/shard_map/ppermute | solution.py:230
  23.6 5.6 %collective-permute-done.16.rest_1_ = bf16[2,512,128]{2,1,0:T(8,128)(2,1)S(1)} collective-permute-done((bf16[2,512,128]{2,1,0:T(8,128)(2,1)S(1)}, bf16[2,512,128]{2,1,0:T(8,128)(2,1)S(1)}, u32[]{:S(2)}, u32[]{:S(2)}) %collective-permute-start.16) | collective-permute-done | bytes 262176 | tf_op jit(solution)/shard_map/ppermute | solution.py:230
  30.7 4.1 %collective-permute-done.12.rest_1_ = bf16[2,512,128]{2,1,0:T(8,128)(2,1)S(1)} collective-permute-done((bf16[2,512,128]{2,1,0:T(8,128)(2,1)S(1)}, bf16[2,512,128]{2,1,0:T(8,128)(2,1)S(1)}, u32[]{:S(2)}, u32[]{:S(2)}) %collective-permute-start.12) | collective-permute-done | bytes 262176 | tf_op jit(solution)/shard_map/ppermute | solution.py:230
  34.8 5.6 %collective-permute-done.8.rest_1_ = bf16[2,512,128]{2,1,0:T(8,128)(2,1)S(1)} collective-permute-done((bf16[2,512,128]{2,1,0:T(8,128)(2,1)S(1)}, bf16[2,512,128]{2,1,0:T(8,128)(2,1)S(1)}, u32[]{:S(2)}, u32[]{:S(2)}) %collective-permute-start.8) | collective-permute-done | bytes 262176 | tf_op jit(solution)/shard_map/ppermute | solution.py:230
  40.4 1.5 %collective-permute-start.25 = (bf16[2,512,128]{2,1,0:T(8,128)(2,1)S(1)}, bf16[2,512,128]{2,1,0:T(8,128)(2,1)S(1)}, u32[]{:S(2)}, u32[]{:S(2)}) collective-permute-start(bf16[2,512,128]{2,1,0:T(8,128)(2,1)S(1)} %get-tuple-element.24), channel_id=1, source_target_pairs={{0,2},{1,3},{2,0},{3,1},{4,6},{5,7},{6,4},{7,5},{8,10},{9,11},{10,... | collective-permute-start | bytes 786440 | tf_op jit(solution)/shard_map/ppermute | solution.py:230
  42.0 4.1 %collective-permute-done.4.rest_1_ = bf16[2,512,128]{2,1,0:T(8,128)(2,1)S(1)} collective-permute-done((bf16[2,512,128]{2,1,0:T(8,128)(2,1)S(1)}, bf16[2,512,128]{2,1,0:T(8,128)(2,1)S(1)}, u32[]{:S(2)}, u32[]{:S(2)}) %collective-permute-start.4) | collective-permute-done | bytes 262176 | tf_op jit(solution)/shard_map/ppermute | solution.py:230
  46.0 4.5 %collective-permute-done.rest_1_ = bf16[2,512,128]{2,1,0:T(8,128)(2,1)S(1)} collective-permute-done((bf16[2,512,128]{2,1,0:T(8,128)(2,1)S(1)}, bf16[2,512,128]{2,1,0:T(8,128)(2,1)S(1)}, u32[]{:S(2)}, u32[]{:S(2)}) %collective-permute-start) | collective-permute-done | bytes 262176 | tf_op jit(solution)/shard_map/ppermute | solution.py:230
  50.5 1.5 %collective-permute-start.21 = (bf16[2,512,128]{2,1,0:T(8,128)(2,1)S(1)}, bf16[2,512,128]{2,1,0:T(8,128)(2,1)S(1)}, u32[]{:S(2)}, u32[]{:S(2)}) collective-permute-start(bf16[2,512,128]{2,1,0:T(8,128)(2,1)S(1)} %get-tuple-element.26), channel_id=1, source_target_pairs={{0,2},{1,3},{2,0},{3,1},{4,6},{5,7},{6,4},{7,5},{8,10},{9,11},{10,... | collective-permute-start | bytes 786440 | tf_op jit(solution)/shard_map/ppermute | solution.py:230
  52.9 1.6 %collective-permute-start.13 = (bf16[2,512,128]{2,1,0:T(8,128)(2,1)S(1)}, bf16[2,512,128]{2,1,0:T(8,128)(2,1)S(1)}, u32[]{:S(2)}, u32[]{:S(2)}) collective-permute-start(bf16[2,512,128]{2,1,0:T(8,128)(2,1)S(1)} %get-tuple-element.30), channel_id=1, source_target_pairs={{0,2},{1,3},{2,0},{3,1},{4,6},{5,7},{6,4},{7,5},{8,10},{9,11},{10,... | collective-permute-start | bytes 786440 | tf_op jit(solution)/shard_map/ppermute | solution.py:230
  54.5 5.2 %collective-permute-done.21.rest_2_ = bf16[2,512,128]{2,1,0:T(8,128)(2,1)S(1)} collective-permute-done((bf16[2,512,128]{2,1,0:T(8,128)(2,1)S(1)}, bf16[2,512,128]{2,1,0:T(8,128)(2,1)S(1)}, u32[]{:S(2)}, u32[]{:S(2)}) %collective-permute-start.21) | collective-permute-done | bytes 262176 | tf_op jit(solution)/shard_map/ppermute | solution.py:230
  59.7 1.5 %collective-permute-start.9 = (bf16[2,512,128]{2,1,0:T(8,128)(2,1)S(1)}, bf16[2,512,128]{2,1,0:T(8,128)(2,1)S(1)}, u32[]{:S(2)}, u32[]{:S(2)}) collective-permute-start(bf16[2,512,128]{2,1,0:T(8,128)(2,1)S(1)} %get-tuple-element.32), channel_id=1, source_target_pairs={{0,2},{1,3},{2,0},{3,1},{4,6},{5,7},{6,4},{7,5},{8,10},{9,11},{10,... | collective-permute-start | bytes 786440 | tf_op jit(solution)/shard_map/ppermute | solution.py:230
  61.2 4.0 %collective-permute-done.17.rest_2_ = bf16[2,512,128]{2,1,0:T(8,128)(2,1)S(1)} collective-permute-done((bf16[2,512,128]{2,1,0:T(8,128)(2,1)S(1)}, bf16[2,512,128]{2,1,0:T(8,128)(2,1)S(1)}, u32[]{:S(2)}, u32[]{:S(2)}) %collective-permute-start.17) | collective-permute-done | bytes 262176 | tf_op jit(solution)/shard_map/ppermute | solution.py:230
  65.3 1.5 %collective-permute-start.5 = (bf16[2,512,128]{2,1,0:T(8,128)(2,1)S(1)}, bf16[2,512,128]{2,1,0:T(8,128)(2,1)S(1)}, u32[]{:S(2)}, u32[]{:S(2)}) collective-permute-start(bf16[2,512,128]{2,1,0:T(8,128)(2,1)S(1)} %get-tuple-element.34), channel_id=1, source_target_pairs={{0,2},{1,3},{2,0},{3,1},{4,6},{5,7},{6,4},{7,5},{8,10},{9,11},{10,... | collective-permute-start | bytes 786440 | tf_op jit(solution)/shard_map/ppermute | solution.py:230
  66.8 4.1 %collective-permute-done.13.rest_2_ = bf16[2,512,128]{2,1,0:T(8,128)(2,1)S(1)} collective-permute-done((bf16[2,512,128]{2,1,0:T(8,128)(2,1)S(1)}, bf16[2,512,128]{2,1,0:T(8,128)(2,1)S(1)}, u32[]{:S(2)}, u32[]{:S(2)}) %collective-permute-start.13) | collective-permute-done | bytes 262176 | tf_op jit(solution)/shard_map/ppermute | solution.py:230
  70.9 1.5 %collective-permute-start.1 = (bf16[2,512,128]{2,1,0:T(8,128)(2,1)S(1)}, bf16[2,512,128]{2,1,0:T(8,128)(2,1)S(1)}, u32[]{:S(2)}, u32[]{:S(2)}) collective-permute-start(bf16[2,512,128]{2,1,0:T(8,128)(2,1)S(1)} %get-tuple-element.36), channel_id=1, source_target_pairs={{0,2},{1,3},{2,0},{3,1},{4,6},{5,7},{6,4},{7,5},{8,10},{9,11},{10,... | collective-permute-start | bytes 786440 | tf_op jit(solution)/shard_map/ppermute | solution.py:230
  72.4 4.1 %collective-permute-done.9.rest_2_ = bf16[2,512,128]{2,1,0:T(8,128)(2,1)S(1)} collective-permute-done((bf16[2,512,128]{2,1,0:T(8,128)(2,1)S(1)}, bf16[2,512,128]{2,1,0:T(8,128)(2,1)S(1)}, u32[]{:S(2)}, u32[]{:S(2)}) %collective-permute-start.9) | collective-permute-done | bytes 262176 | tf_op jit(solution)/shard_map/ppermute | solution.py:230
  76.5 5.6 %collective-permute-done.5.rest_2_ = bf16[2,512,128]{2,1,0:T(8,128)(2,1)S(1)} collective-permute-done((bf16[2,512,128]{2,1,0:T(8,128)(2,1)S(1)}, bf16[2,512,128]{2,1,0:T(8,128)(2,1)S(1)}, u32[]{:S(2)}, u32[]{:S(2)}) %collective-permute-start.5) | collective-permute-done | bytes 262176 | tf_op jit(solution)/shard_map/ppermute | solution.py:230
  82.7 3.1 %collective-permute-done.1.rest_0_ = bf16[2,512,128]{2,1,0:T(8,128)(2,1)S(1)} collective-permute-done((bf16[2,512,128]{2,1,0:T(8,128)(2,1)S(1)}, bf16[2,512,128]{2,1,0:T(8,128)(2,1)S(1)}, u32[]{:S(2)}, u32[]{:S(2)}) %collective-permute-start.1) | collective-permute-done | bytes 262176 | tf_op jit(solution)/shard_map/ppermute | solution.py:230
  85.8 1.7 %shard_map.38 = (f32[4,144,256]{2,1,0:T(8,128)S(1)}, f32[4,8,256]{2,1,0:T(8,128)S(1)}) custom-call(bf16[256,4096]{1,0:T(8,128)(2,1)S(1)} %copy-done, bf16[2,512,128]{2,1,0:T(8,128)(2,1)S(1)} %shard_map.37.rest_0_, bf16[2,512,128]{2,1,0:T(8,128)(2,1)S(1)} %collective-permute-done.rest_1_, bf16[2,512,128]{2,1,0:T(8,128)(2,1)S(1)} %collective-permute-done.3.rest_2_), custom_call_target="tpu_custom_call" | custom-call | flops 402653184 | bytes 1310720 | tf_op jit(solution)/shard_map/pallas_call | solution.py:185
  89.5 3.3 %shard_map.47.rest_5_ = bf16[256,4096]{1,0:T(8,128)(2,1)} custom-call(bf16[256,4096]{1,0:T(8,128)(2,1)S(1)} %copy-done, bf16[2,512,128]{2,1,0:T(8,128)(2,1)S(1)} %shard_map.46.rest_0_, bf16[2,512,128]{2,1,0:T(8,128)(2,1)S(1)} %collective-permute-done.28.rest_1_, bf16[2,512,128]{2,1,0:T(8,128)(2,1)S(1)} %collective-permute-done.29.rest_2_, ...), custom_call_target="tpu_custom_call" | custom-call | flops 671088640 | bytes 1835008 | tf_op jit(solution)/shard_map/pallas_call | solution.py:185
  93.3 3.1 %shard_map.48.rest_5_ = bf16[256,4096]{1,0:T(8,128)(2,1)} custom-call(bf16[256,4096]{1,0:T(8,128)(2,1)S(1)} %copy-done, bf16[2,512,128]{2,1,0:T(8,128)(2,1)S(1)} %shard_map.45.rest_0_, bf16[2,512,128]{2,1,0:T(8,128)(2,1)S(1)} %collective-permute-done.24.rest_1_, ...), custom_call_target="tpu_custom_call", output_to_operand_aliasing={{}: (6, {})} | custom-call | flops 671088640 | bytes 1835008 | tf_op jit(solution)/shard_map/pallas_call | solution.py:185
  96.8 3.1 %shard_map.49.rest_5_ = bf16[256,4096]{1,0:T(8,128)(2,1)} custom-call(bf16[256,4096]{1,0:T(8,128)(2,1)S(1)} %copy-done, bf16[2,512,128]{2,1,0:T(8,128)(2,1)S(1)} %shard_map.44.rest_0_, bf16[2,512,128]{2,1,0:T(8,128)(2,1)S(1)} %collective-permute-done.20.rest_1_, ...), custom_call_target="tpu_custom_call", output_to_operand_aliasing={{}: (6, {})} | custom-call | flops 671088640 | bytes 1835008 | tf_op jit(solution)/shard_map/pallas_call | solution.py:185
  99.9 3.1 %shard_map.50.rest_5_ = bf16[256,4096]{1,0:T(8,128)(2,1)} custom-call(bf16[256,4096]{1,0:T(8,128)(2,1)S(1)} %copy-done, bf16[2,512,128]{2,1,0:T(8,128)(2,1)S(1)} %shard_map.43.rest_0_, bf16[2,512,128]{2,1,0:T(8,128)(2,1)S(1)} %collective-permute-done.16.rest_1_, ...), custom_call_target="tpu_custom_call", output_to_operand_aliasing={{}: (6, {})} | custom-call | flops 671088640 | bytes 1835008 | tf_op jit(solution)/shard_map/pallas_call | solution.py:185
  103.0 3.1 %shard_map.51.rest_5_ = bf16[256,4096]{1,0:T(8,128)(2,1)} custom-call(bf16[256,4096]{1,0:T(8,128)(2,1)S(1)} %copy-done, bf16[2,512,128]{2,1,0:T(8,128)(2,1)S(1)} %shard_map.42.rest_0_, bf16[2,512,128]{2,1,0:T(8,128)(2,1)S(1)} %collective-permute-done.12.rest_1_, ...), custom_call_target="tpu_custom_call", output_to_operand_aliasing={{}: (6, {})} | custom-call | flops 671088640 | bytes 1835008 | tf_op jit(solution)/shard_map/pallas_call | solution.py:185
  106.1 3.1 %shard_map.52.rest_5_ = bf16[256,4096]{1,0:T(8,128)(2,1)} custom-call(bf16[256,4096]{1,0:T(8,128)(2,1)S(1)} %copy-done, bf16[2,512,128]{2,1,0:T(8,128)(2,1)S(1)} %shard_map.41.rest_0_, bf16[2,512,128]{2,1,0:T(8,128)(2,1)S(1)} %collective-permute-done.8.rest_1_, ...), custom_call_target="tpu_custom_call", output_to_operand_aliasing={{}: (6, {})} | custom-call | flops 671088640 | bytes 1835008 | tf_op jit(solution)/shard_map/pallas_call | solution.py:185
  109.2 3.1 %shard_map.53.rest_3_ = bf16[256,4096]{1,0:T(8,128)(2,1)} custom-call(bf16[256,4096]{1,0:T(8,128)(2,1)S(1)} %copy-done, bf16[2,512,128]{2,1,0:T(8,128)(2,1)S(1)} %shard_map.40.rest_0_, bf16[2,512,128]{2,1,0:T(8,128)(2,1)S(1)} %collective-permute-done.4.rest_1_, ...), custom_call_target="tpu_custom_call", output_to_operand_aliasing={{}: (6, {})} | custom-call | flops 671088640 | bytes 1835008 | tf_op jit(solution)/shard_map/pallas_call | solution.py:185
  112.3 2.1 %shard_map.54 = bf16[256,4096]{1,0:T(8,128)(2,1)} custom-call(bf16[256,4096]{1,0:T(8,128)(2,1)S(1)} %copy-done, bf16[2,512,128]{2,1,0:T(8,128)(2,1)S(1)} %collective-permute-done.2.rest_0_, f32[4,144,256]{2,1,0:T(8,128)S(1)} %get-tuple-element.19.rest_1_, f32[4,8,256]{2,1,0:T(8,128)S(1)} %get-tuple-element.20.rest_2_, ...), custom_call_target="tpu_custom_call", output_to_operand_aliasing={{}: (4, {})} | custom-call | flops 134217728 | bytes 786432 | tf_op jit(solution)/shard_map/pallas_call | solution.py:185
  (64 shorter events, 9.6 us)
Async XLA Ops:
  1.2 11.1 %collective-permute-start.28 = (bf16[2,512,128]{2,1,0:T(8,128)(2,1)S(1)}, bf16[2,512,128]{2,1,0:T(8,128)(2,1)S(1)}, u32[]{:S(2)}, u32[]{:S(2)}) collective-permute-start(bf16[2,512,128]{2,1,0:T(8,128)(2,1)S(1)} %shard_map.46.rest_0_), channel_id=1, source_target_pairs={{0,4},{1,5},{2,6},{3,7},{4,8},{5,9},{6,10},{7,11},{8,12},{9,13},{1... | collective-permute-start | bytes 786440 | tf_op jit(solution)/shard_map/ppermute | solution.py:230
  2.7 15.2 %collective-permute-start.24 = (bf16[2,512,128]{2,1,0:T(8,128)(2,1)S(1)}, bf16[2,512,128]{2,1,0:T(8,128)(2,1)S(1)}, u32[]{:S(2)}, u32[]{:S(2)}) collective-permute-start(bf16[2,512,128]{2,1,0:T(8,128)(2,1)S(1)} %shard_map.45.rest_0_), channel_id=1, source_target_pairs={{0,4},{1,5},{2,6},{3,7},{4,8},{5,9},{6,10},{7,11},{8,12},{9,13},{1... | collective-permute-start | bytes 786440 | tf_op jit(solution)/shard_map/ppermute | solution.py:230
  5.3 18.3 %collective-permute-start.20 = (bf16[2,512,128]{2,1,0:T(8,128)(2,1)S(1)}, bf16[2,512,128]{2,1,0:T(8,128)(2,1)S(1)}, u32[]{:S(2)}, u32[]{:S(2)}) collective-permute-start(bf16[2,512,128]{2,1,0:T(8,128)(2,1)S(1)} %shard_map.44.rest_0_), channel_id=1, source_target_pairs={{0,4},{1,5},{2,6},{3,7},{4,8},{5,9},{6,10},{7,11},{8,12},{9,13},{1... | collective-permute-start | bytes 786440 | tf_op jit(solution)/shard_map/ppermute | solution.py:230
  7.0 22.1 %collective-permute-start.16 = (bf16[2,512,128]{2,1,0:T(8,128)(2,1)S(1)}, bf16[2,512,128]{2,1,0:T(8,128)(2,1)S(1)}, u32[]{:S(2)}, u32[]{:S(2)}) collective-permute-start(bf16[2,512,128]{2,1,0:T(8,128)(2,1)S(1)} %shard_map.43.rest_0_), channel_id=1, source_target_pairs={{0,4},{1,5},{2,6},{3,7},{4,8},{5,9},{6,10},{7,11},{8,12},{9,13},{1... | collective-permute-start | bytes 786440 | tf_op jit(solution)/shard_map/ppermute | solution.py:230
  8.8 26.0 %collective-permute-start.12 = (bf16[2,512,128]{2,1,0:T(8,128)(2,1)S(1)}, bf16[2,512,128]{2,1,0:T(8,128)(2,1)S(1)}, u32[]{:S(2)}, u32[]{:S(2)}) collective-permute-start(bf16[2,512,128]{2,1,0:T(8,128)(2,1)S(1)} %shard_map.42.rest_0_), channel_id=1, source_target_pairs={{0,4},{1,5},{2,6},{3,7},{4,8},{5,9},{6,10},{7,11},{8,12},{9,13},{1... | collective-permute-start | bytes 786440 | tf_op jit(solution)/shard_map/ppermute | solution.py:230
  12.3 28.1 %collective-permute-start.8 = (bf16[2,512,128]{2,1,0:T(8,128)(2,1)S(1)}, bf16[2,512,128]{2,1,0:T(8,128)(2,1)S(1)}, u32[]{:S(2)}, u32[]{:S(2)}) collective-permute-start(bf16[2,512,128]{2,1,0:T(8,128)(2,1)S(1)} %shard_map.41.rest_0_), channel_id=1, source_target_pairs={{0,4},{1,5},{2,6},{3,7},{4,8},{5,9},{6,10},{7,11},{8,12},{9,13},{1... | collective-permute-start | bytes 786440 | tf_op jit(solution)/shard_map/ppermute | solution.py:230
  17.9 28.1 %collective-permute-start.4 = (bf16[2,512,128]{2,1,0:T(8,128)(2,1)S(1)}, bf16[2,512,128]{2,1,0:T(8,128)(2,1)S(1)}, u32[]{:S(2)}, u32[]{:S(2)}) collective-permute-start(bf16[2,512,128]{2,1,0:T(8,128)(2,1)S(1)} %shard_map.40.rest_0_), channel_id=1, source_target_pairs={{0,4},{1,5},{2,6},{3,7},{4,8},{5,9},{6,10},{7,11},{8,12},{9,13},{1... | collective-permute-start | bytes 786440 | tf_op jit(solution)/shard_map/ppermute | solution.py:230
  23.5 27.0 %collective-permute-start = (bf16[2,512,128]{2,1,0:T(8,128)(2,1)S(1)}, bf16[2,512,128]{2,1,0:T(8,128)(2,1)S(1)}, u32[]{:S(2)}, u32[]{:S(2)}) collective-permute-start(bf16[2,512,128]{2,1,0:T(8,128)(2,1)S(1)} %shard_map.37.rest_0_), channel_id=1, source_target_pairs={{0,4},{1,5},{2,6},{3,7},{4,8},{5,9},{6,10},{7,11},{8,12},{9,13},{1... | collective-permute-start | bytes 786440 | tf_op jit(solution)/shard_map/ppermute | solution.py:230
  29.2 22.9 %collective-permute-start.29 = (bf16[2,512,128]{2,1,0:T(8,128)(2,1)S(1)}, bf16[2,512,128]{2,1,0:T(8,128)(2,1)S(1)}, u32[]{:S(2)}, u32[]{:S(2)}) collective-permute-start(bf16[2,512,128]{2,1,0:T(8,128)(2,1)S(1)} %get-tuple-element.22), channel_id=1, source_target_pairs={{0,2},{1,3},{2,0},{3,1},{4,6},{5,7},{6,4},{7,5},{8,10},{9,11},{10,... | collective-permute-start | bytes 786440 | tf_op jit(solution)/shard_map/ppermute | solution.py:230
  34.8 17.3 %collective-permute-start.30 = (bf16[2,512,128]{2,1,0:T(8,128)(2,1)S(1)}, bf16[2,512,128]{2,1,0:T(8,128)(2,1)S(1)}, u32[]{:S(2)}, u32[]{:S(2)}) collective-permute-start(bf16[2,512,128]{2,1,0:T(8,128)(2,1)S(1)} %get-tuple-element.21), channel_id=1, source_target_pairs={{0,1},{1,0},{2,3},{3,2},{4,5},{5,4},{6,7},{7,6},{8,9},{9,8},{10,11... | collective-permute-start | bytes 786440 | tf_op jit(solution)/shard_map/ppermute | solution.py:230
  40.4 12.3 %collective-permute-start.25 = (bf16[2,512,128]{2,1,0:T(8,128)(2,1)S(1)}, bf16[2,512,128]{2,1,0:T(8,128)(2,1)S(1)}, u32[]{:S(2)}, u32[]{:S(2)}) collective-permute-start(bf16[2,512,128]{2,1,0:T(8,128)(2,1)S(1)} %get-tuple-element.24), channel_id=1, source_target_pairs={{0,2},{1,3},{2,0},{3,1},{4,6},{5,7},{6,4},{7,5},{8,10},{9,11},{10,... | collective-permute-start | bytes 786440 | tf_op jit(solution)/shard_map/ppermute | solution.py:230
  46.0 6.9 %collective-permute-start.26 = (bf16[2,512,128]{2,1,0:T(8,128)(2,1)S(1)}, bf16[2,512,128]{2,1,0:T(8,128)(2,1)S(1)}, u32[]{:S(2)}, u32[]{:S(2)}) collective-permute-start(bf16[2,512,128]{2,1,0:T(8,128)(2,1)S(1)} %get-tuple-element.23), channel_id=1, source_target_pairs={{0,1},{1,0},{2,3},{3,2},{4,5},{5,4},{6,7},{7,6},{8,9},{9,8},{10,11... | collective-permute-start | bytes 786440 | tf_op jit(solution)/shard_map/ppermute | solution.py:230
  50.5 9.2 %collective-permute-start.21 = (bf16[2,512,128]{2,1,0:T(8,128)(2,1)S(1)}, bf16[2,512,128]{2,1,0:T(8,128)(2,1)S(1)}, u32[]{:S(2)}, u32[]{:S(2)}) collective-permute-start(bf16[2,512,128]{2,1,0:T(8,128)(2,1)S(1)} %get-tuple-element.26), channel_id=1, source_target_pairs={{0,2},{1,3},{2,0},{3,1},{4,6},{5,7},{6,4},{7,5},{8,10},{9,11},{10,... | collective-permute-start | bytes 786440 | tf_op jit(solution)/shard_map/ppermute | solution.py:230
  52.0 7.7 %collective-permute-start.22 = (bf16[2,512,128]{2,1,0:T(8,128)(2,1)S(1)}, bf16[2,512,128]{2,1,0:T(8,128)(2,1)S(1)}, u32[]{:S(2)}, u32[]{:S(2)}) collective-permute-start(bf16[2,512,128]{2,1,0:T(8,128)(2,1)S(1)} %get-tuple-element.25), channel_id=1, source_target_pairs={{0,1},{1,0},{2,3},{3,2},{4,5},{5,4},{6,7},{7,6},{8,9},{9,8},{10,11... | collective-permute-start | bytes 786440 | tf_op jit(solution)/shard_map/ppermute | solution.py:230
  52.1 13.2 %collective-permute-start.17 = (bf16[2,512,128]{2,1,0:T(8,128)(2,1)S(1)}, bf16[2,512,128]{2,1,0:T(8,128)(2,1)S(1)}, u32[]{:S(2)}, u32[]{:S(2)}) collective-permute-start(bf16[2,512,128]{2,1,0:T(8,128)(2,1)S(1)} %get-tuple-element.28), channel_id=1, source_target_pairs={{0,2},{1,3},{2,0},{3,1},{4,6},{5,7},{6,4},{7,5},{8,10},{9,11},{10,... | collective-permute-start | bytes 786440 | tf_op jit(solution)/shard_map/ppermute | solution.py:230
  52.7 14.2 %collective-permute-start.18 = (bf16[2,512,128]{2,1,0:T(8,128)(2,1)S(1)}, bf16[2,512,128]{2,1,0:T(8,128)(2,1)S(1)}, u32[]{:S(2)}, u32[]{:S(2)}) collective-permute-start(bf16[2,512,128]{2,1,0:T(8,128)(2,1)S(1)} %get-tuple-element.27), channel_id=1, source_target_pairs={{0,1},{1,0},{2,3},{3,2},{4,5},{5,4},{6,7},{7,6},{8,9},{9,8},{10,11... | collective-permute-start | bytes 786440 | tf_op jit(solution)/shard_map/ppermute | solution.py:230
  52.9 18.0 %collective-permute-start.13 = (bf16[2,512,128]{2,1,0:T(8,128)(2,1)S(1)}, bf16[2,512,128]{2,1,0:T(8,128)(2,1)S(1)}, u32[]{:S(2)}, u32[]{:S(2)}) collective-permute-start(bf16[2,512,128]{2,1,0:T(8,128)(2,1)S(1)} %get-tuple-element.30), channel_id=1, source_target_pairs={{0,2},{1,3},{2,0},{3,1},{4,6},{5,7},{6,4},{7,5},{8,10},{9,11},{10,... | collective-permute-start | bytes 786440 | tf_op jit(solution)/shard_map/ppermute | solution.py:230
  59.7 12.8 %collective-permute-start.14 = (bf16[2,512,128]{2,1,0:T(8,128)(2,1)S(1)}, bf16[2,512,128]{2,1,0:T(8,128)(2,1)S(1)}, u32[]{:S(2)}, u32[]{:S(2)}) collective-permute-start(bf16[2,512,128]{2,1,0:T(8,128)(2,1)S(1)} %get-tuple-element.29), channel_id=1, source_target_pairs={{0,1},{1,0},{2,3},{3,2},{4,5},{5,4},{6,7},{7,6},{8,9},{9,8},{10,11... | collective-permute-start | bytes 786440 | tf_op jit(solution)/shard_map/ppermute | solution.py:230
  59.7 16.8 %collective-permute-start.9 = (bf16[2,512,128]{2,1,0:T(8,128)(2,1)S(1)}, bf16[2,512,128]{2,1,0:T(8,128)(2,1)S(1)}, u32[]{:S(2)}, u32[]{:S(2)}) collective-permute-start(bf16[2,512,128]{2,1,0:T(8,128)(2,1)S(1)} %get-tuple-element.32), channel_id=1, source_target_pairs={{0,2},{1,3},{2,0},{3,1},{4,6},{5,7},{6,4},{7,5},{8,10},{9,11},{10,... | collective-permute-start | bytes 786440 | tf_op jit(solution)/shard_map/ppermute | solution.py:230
  65.3 16.9 %collective-permute-start.5 = (bf16[2,512,128]{2,1,0:T(8,128)(2,1)S(1)}, bf16[2,512,128]{2,1,0:T(8,128)(2,1)S(1)}, u32[]{:S(2)}, u32[]{:S(2)}) collective-permute-start(bf16[2,512,128]{2,1,0:T(8,128)(2,1)S(1)} %get-tuple-element.34), channel_id=1, source_target_pairs={{0,2},{1,3},{2,0},{3,1},{4,6},{5,7},{6,4},{7,5},{8,10},{9,11},{10,... | collective-permute-start | bytes 786440 | tf_op jit(solution)/shard_map/ppermute | solution.py:230
  66.8 15.3 %collective-permute-start.3 = (bf16[2,512,128]{2,1,0:T(8,128)(2,1)S(1)}, bf16[2,512,128]{2,1,0:T(8,128)(2,1)S(1)}, u32[]{:S(2)}, u32[]{:S(2)}) collective-permute-start(bf16[2,512,128]{2,1,0:T(8,128)(2,1)S(1)} %get-tuple-element.35), channel_id=1, source_target_pairs={{0,1},{1,0},{2,3},{3,2},{4,5},{5,4},{6,7},{7,6},{8,9},{9,8},{10,11... | collective-permute-start | bytes 786440 | tf_op jit(solution)/shard_map/ppermute | solution.py:230
  70.9 14.9 %collective-permute-start.1 = (bf16[2,512,128]{2,1,0:T(8,128)(2,1)S(1)}, bf16[2,512,128]{2,1,0:T(8,128)(2,1)S(1)}, u32[]{:S(2)}, u32[]{:S(2)}) collective-permute-start(bf16[2,512,128]{2,1,0:T(8,128)(2,1)S(1)} %get-tuple-element.36), channel_id=1, source_target_pairs={{0,2},{1,3},{2,0},{3,1},{4,6},{5,7},{6,4},{7,5},{8,10},{9,11},{10,... | collective-permute-start | bytes 786440 | tf_op jit(solution)/shard_map/ppermute | solution.py:230
  72.4 16.4 %collective-permute-start.31 = (bf16[2,512,128]{2,1,0:T(8,128)(2,1)S(1)}, bf16[2,512,128]{2,1,0:T(8,128)(2,1)S(1)}, u32[]{:S(2)}, u32[]{:S(2)}) collective-permute-start(bf16[2,512,128]{2,1,0:T(8,128)(2,1)S(1)} %collective-permute-done.29.rest_2_), channel_id=1, source_target_pairs={{0,1},{1,0},{2,3},{3,2},{4,5},{5,4},{6,7},{7,6},{8,9},{9,8},{10,11... | collective-permute-start | bytes 786440 | tf_op jit(solution)/shard_map/ppermute | solution.py:230
  76.5 12.9 %collective-permute-start.27 = (bf16[2,512,128]{2,1,0:T(8,128)(2,1)S(1)}, bf16[2,512,128]{2,1,0:T(8,128)(2,1)S(1)}, u32[]{:S(2)}, u32[]{:S(2)}) collective-permute-start(bf16[2,512,128]{2,1,0:T(8,128)(2,1)S(1)} %collective-permute-done.25.rest_2_), channel_id=1, source_target_pairs={{0,1},{1,0},{2,3},{3,2},{4,5},{5,4},{6,7},{7,6},{8,9},{9,8},{10,11... | collective-permute-start | bytes 786440 | tf_op jit(solution)/shard_map/ppermute | solution.py:230
  82.1 10.6 %collective-permute-start.23 = (bf16[2,512,128]{2,1,0:T(8,128)(2,1)S(1)}, bf16[2,512,128]{2,1,0:T(8,128)(2,1)S(1)}, u32[]{:S(2)}, u32[]{:S(2)}) collective-permute-start(bf16[2,512,128]{2,1,0:T(8,128)(2,1)S(1)} %collective-permute-done.21.rest_2_), channel_id=1, source_target_pairs={{0,1},{1,0},{2,3},{3,2},{4,5},{5,4},{6,7},{7,6},{8,9},{9,8},{10,11... | collective-permute-start | bytes 786440 | tf_op jit(solution)/shard_map/ppermute | solution.py:230
  82.2 11.1 %collective-permute-start.19 = (bf16[2,512,128]{2,1,0:T(8,128)(2,1)S(1)}, bf16[2,512,128]{2,1,0:T(8,128)(2,1)S(1)}, u32[]{:S(2)}, u32[]{:S(2)}) collective-permute-start(bf16[2,512,128]{2,1,0:T(8,128)(2,1)S(1)} %collective-permute-done.17.rest_2_), channel_id=1, source_target_pairs={{0,1},{1,0},{2,3},{3,2},{4,5},{5,4},{6,7},{7,6},{8,9},{9,8},{10,11... | collective-permute-start | bytes 786440 | tf_op jit(solution)/shard_map/ppermute | solution.py:230
  85.8 10.6 %collective-permute-start.15 = (bf16[2,512,128]{2,1,0:T(8,128)(2,1)S(1)}, bf16[2,512,128]{2,1,0:T(8,128)(2,1)S(1)}, u32[]{:S(2)}, u32[]{:S(2)}) collective-permute-start(bf16[2,512,128]{2,1,0:T(8,128)(2,1)S(1)} %collective-permute-done.13.rest_2_), channel_id=1, source_target_pairs={{0,1},{1,0},{2,3},{3,2},{4,5},{5,4},{6,7},{7,6},{8,9},{9,8},{10,11... | collective-permute-start | bytes 786440 | tf_op jit(solution)/shard_map/ppermute | solution.py:230
  88.9 17.2 %collective-permute-start.10 = (bf16[2,512,128]{2,1,0:T(8,128)(2,1)S(1)}, bf16[2,512,128]{2,1,0:T(8,128)(2,1)S(1)}, u32[]{:S(2)}, u32[]{:S(2)}) collective-permute-start(bf16[2,512,128]{2,1,0:T(8,128)(2,1)S(1)} %get-tuple-element.31), channel_id=1, source_target_pairs={{0,1},{1,0},{2,3},{3,2},{4,5},{5,4},{6,7},{7,6},{8,9},{9,8},{10,11... | collective-permute-start | bytes 786440 | tf_op jit(solution)/shard_map/ppermute | solution.py:230
  89.4 16.7 %collective-permute-start.11 = (bf16[2,512,128]{2,1,0:T(8,128)(2,1)S(1)}, bf16[2,512,128]{2,1,0:T(8,128)(2,1)S(1)}, u32[]{:S(2)}, u32[]{:S(2)}) collective-permute-start(bf16[2,512,128]{2,1,0:T(8,128)(2,1)S(1)} %collective-permute-done.9.rest_2_), channel_id=1, source_target_pairs={{0,1},{1,0},{2,3},{3,2},{4,5},{5,4},{6,7},{7,6},{8,9},{9,8},{10,11... | collective-permute-start | bytes 786440 | tf_op jit(solution)/shard_map/ppermute | solution.py:230
  92.8 16.4 %collective-permute-start.6 = (bf16[2,512,128]{2,1,0:T(8,128)(2,1)S(1)}, bf16[2,512,128]{2,1,0:T(8,128)(2,1)S(1)}, u32[]{:S(2)}, u32[]{:S(2)}) collective-permute-start(bf16[2,512,128]{2,1,0:T(8,128)(2,1)S(1)} %get-tuple-element.33), channel_id=1, source_target_pairs={{0,1},{1,0},{2,3},{3,2},{4,5},{5,4},{6,7},{7,6},{8,9},{9,8},{10,11... | collective-permute-start | bytes 786440 | tf_op jit(solution)/shard_map/ppermute | solution.py:230
  93.2 16.0 %collective-permute-start.7 = (bf16[2,512,128]{2,1,0:T(8,128)(2,1)S(1)}, bf16[2,512,128]{2,1,0:T(8,128)(2,1)S(1)}, u32[]{:S(2)}, u32[]{:S(2)}) collective-permute-start(bf16[2,512,128]{2,1,0:T(8,128)(2,1)S(1)} %collective-permute-done.5.rest_2_), channel_id=1, source_target_pairs={{0,1},{1,0},{2,3},{3,2},{4,5},{5,4},{6,7},{7,6},{8,9},{9,8},{10,11... | collective-permute-start | bytes 786440 | tf_op jit(solution)/shard_map/ppermute | solution.py:230
  96.4 15.9 %collective-permute-start.2 = (bf16[2,512,128]{2,1,0:T(8,128)(2,1)S(1)}, bf16[2,512,128]{2,1,0:T(8,128)(2,1)S(1)}, u32[]{:S(2)}, u32[]{:S(2)}) collective-permute-start(bf16[2,512,128]{2,1,0:T(8,128)(2,1)S(1)} %collective-permute-done.1.rest_0_), channel_id=1, source_target_pairs={{0,1},{1,0},{2,3},{3,2},{4,5},{5,4},{6,7},{7,6},{8,9},{9,8},{10,11... | collective-permute-start | bytes 786440 | tf_op jit(solution)/shard_map/ppermute | solution.py:230
  (3 other events, 50.5 us)
where the time goes:
time: 115 us; the launch traced here: 114 us
  waiting for transfers between devices  64.2 us (56%)
  Pallas kernels  29 us (25%)
  starting transfers between devices  20.7 us (18%)
    ppermute x32, waiting for transfers between devices, send(): return lax.ppermute(piece, 'seq', pairs)  64.2 us
    pallas_call x10, Pallas kernels, attend(): pl.pallas_call(functools.partial(attend_kernel, parts, early, bool(before...  26.9 us
    ppermute x32, starting transfers between devices, send(): return lax.ppermute(piece, 'seq', pairs)  20.7 us
  transfers between devices with their start and end apart: 32, of which 14 were waited for; matrix products, arithmetic and copies ran while one was open for 0% of the time, Pallas kernels for 22%

commit v1 on v0

--- a/solution.py
+++ b/solution.py
@@ -243,11 +243,8 @@
             before = attend(
                 queries, (mine, distant, pair1), first, heads, None, parts=(0, 2), early=True
             )
-            before = attend(
-                queries, (middle,), first, heads, None, parts=(1,), early=True, before=before
-            )
-            pieces = (pair2,)
-            options = {"parts": (3,), "before": before}
+            pieces = (middle, pair2)
+            options = {"parts": (1, 3), "before": before}
         output = attend(queries, pieces, first, heads, output, **options)
     return output
 

time: 115 us -> 114 us (level)
  Pallas kernels: 29 us -> 27.7 us
    pallas_call x10 -> x9, Pallas kernels: 26.9 us -> 25.7 us  [attend(): pl.pallas_call(functools.partial(attend_kernel, parts, early, bool(before...]
  transfers between devices with their start and end apart: 32 -> 32, of which waited for: 14 -> 14; matrix products, arithmetic and copies ran while one was open for 0% -> 0% of each run, Pallas kernels for 22% -> 21%
where the time goes in v1:
time: 114 us; the launch traced here: 113 us
  waiting for transfers between devices  64.2 us (56%)
  Pallas kernels  27.7 us (24%)
  starting transfers between devices  20.7 us (18%)
    ppermute x32, waiting for transfers between devices, send(): return lax.ppermute(piece, 'seq', pairs)  64.2 us
    pallas_call x9, Pallas kernels, attend(): pl.pallas_call(functools.partial(attend_kernel, parts, early, bool(before...  25.7 us
    ppermute x32, starting transfers between devices, send(): return lax.ppermute(piece, 'seq', pairs)  20.7 us
  transfers between devices with their start and end apart: 32, of which 14 were waited for; matrix products, arithmetic and copies ran while one was open for 0% of the time, Pallas kernels for 21%

profile of v1, /device:TPU:26, one launch (start us, length us, event | category | flops | bytes accessed | tf_op | source)
XLA Modules:
  0.0 113.2 jit_solution(7814676623635191312)
XLA Ops:
  2.7 2.5 %collective-permute-start.24 = (bf16[2,512,128]{2,1,0:T(8,128)(2,1)S(1)}, bf16[2,512,128]{2,1,0:T(8,128)(2,1)S(1)}, u32[]{:S(2)}, u32[]{:S(2)}) collective-permute-start(bf16[2,512,128]{2,1,0:T(8,128)(2,1)S(1)} %shard_map.44.rest_0_), channel_id=1, source_target_pairs={{0,4},{1,5},{2,6},{3,7},{4,8},{5,9},{6,10},{7,11},{8,12},{9,13},{1... | collective-permute-start | bytes 786440 | tf_op jit(solution)/shard_map/ppermute | solution.py:230
  5.3 1.6 %collective-permute-start.20 = (bf16[2,512,128]{2,1,0:T(8,128)(2,1)S(1)}, bf16[2,512,128]{2,1,0:T(8,128)(2,1)S(1)}, u32[]{:S(2)}, u32[]{:S(2)}) collective-permute-start(bf16[2,512,128]{2,1,0:T(8,128)(2,1)S(1)} %shard_map.43.rest_0_), channel_id=1, source_target_pairs={{0,4},{1,5},{2,6},{3,7},{4,8},{5,9},{6,10},{7,11},{8,12},{9,13},{1... | collective-permute-start | bytes 786440 | tf_op jit(solution)/shard_map/ppermute | solution.py:230
  7.0 1.6 %collective-permute-start.16 = (bf16[2,512,128]{2,1,0:T(8,128)(2,1)S(1)}, bf16[2,512,128]{2,1,0:T(8,128)(2,1)S(1)}, u32[]{:S(2)}, u32[]{:S(2)}) collective-permute-start(bf16[2,512,128]{2,1,0:T(8,128)(2,1)S(1)} %shard_map.42.rest_0_), channel_id=1, source_target_pairs={{0,4},{1,5},{2,6},{3,7},{4,8},{5,9},{6,10},{7,11},{8,12},{9,13},{1... | collective-permute-start | bytes 786440 | tf_op jit(solution)/shard_map/ppermute | solution.py:230
  9.2 3.1 %collective-permute-done.28.rest_1_ = bf16[2,512,128]{2,1,0:T(8,128)(2,1)S(1)} collective-permute-done((bf16[2,512,128]{2,1,0:T(8,128)(2,1)S(1)}, bf16[2,512,128]{2,1,0:T(8,128)(2,1)S(1)}, u32[]{:S(2)}, u32[]{:S(2)}) %collective-permute-start.28) | collective-permute-done | bytes 262176 | tf_op jit(solution)/shard_map/ppermute | solution.py:230
  12.4 5.6 %collective-permute-done.24.rest_1_ = bf16[2,512,128]{2,1,0:T(8,128)(2,1)S(1)} collective-permute-done((bf16[2,512,128]{2,1,0:T(8,128)(2,1)S(1)}, bf16[2,512,128]{2,1,0:T(8,128)(2,1)S(1)}, u32[]{:S(2)}, u32[]{:S(2)}) %collective-permute-start.24) | collective-permute-done | bytes 262176 | tf_op jit(solution)/shard_map/ppermute | solution.py:230
  18.0 5.6 %collective-permute-done.20.rest_1_ = bf16[2,512,128]{2,1,0:T(8,128)(2,1)S(1)} collective-permute-done((bf16[2,512,128]{2,1,0:T(8,128)(2,1)S(1)}, bf16[2,512,128]{2,1,0:T(8,128)(2,1)S(1)}, u32[]{:S(2)}, u32[]{:S(2)}) %collective-permute-start.20) | collective-permute-done | bytes 262176 | tf_op jit(solution)/shard_map/ppermute | solution.py:230
  23.6 5.6 %collective-permute-done.16.rest_1_ = bf16[2,512,128]{2,1,0:T(8,128)(2,1)S(1)} collective-permute-done((bf16[2,512,128]{2,1,0:T(8,128)(2,1)S(1)}, bf16[2,512,128]{2,1,0:T(8,128)(2,1)S(1)}, u32[]{:S(2)}, u32[]{:S(2)}) %collective-permute-start.16) | collective-permute-done | bytes 262176 | tf_op jit(solution)/shard_map/ppermute | solution.py:230
  30.7 4.1 %collective-permute-done.12.rest_1_ = bf16[2,512,128]{2,1,0:T(8,128)(2,1)S(1)} collective-permute-done((bf16[2,512,128]{2,1,0:T(8,128)(2,1)S(1)}, bf16[2,512,128]{2,1,0:T(8,128)(2,1)S(1)}, u32[]{:S(2)}, u32[]{:S(2)}) %collective-permute-start.12) | collective-permute-done | bytes 262176 | tf_op jit(solution)/shard_map/ppermute | solution.py:230
  34.8 5.6 %collective-permute-done.8.rest_1_ = bf16[2,512,128]{2,1,0:T(8,128)(2,1)S(1)} collective-permute-done((bf16[2,512,128]{2,1,0:T(8,128)(2,1)S(1)}, bf16[2,512,128]{2,1,0:T(8,128)(2,1)S(1)}, u32[]{:S(2)}, u32[]{:S(2)}) %collective-permute-start.8) | collective-permute-done | bytes 262176 | tf_op jit(solution)/shard_map/ppermute | solution.py:230
  40.4 1.5 %collective-permute-start.25 = (bf16[2,512,128]{2,1,0:T(8,128)(2,1)S(1)}, bf16[2,512,128]{2,1,0:T(8,128)(2,1)S(1)}, u32[]{:S(2)}, u32[]{:S(2)}) collective-permute-start(bf16[2,512,128]{2,1,0:T(8,128)(2,1)S(1)} %get-tuple-element.20), channel_id=1, source_target_pairs={{0,2},{1,3},{2,0},{3,1},{4,6},{5,7},{6,4},{7,5},{8,10},{9,11},{10,... | collective-permute-start | bytes 786440 | tf_op jit(solution)/shard_map/ppermute | solution.py:230
  42.0 4.1 %collective-permute-done.4.rest_1_ = bf16[2,512,128]{2,1,0:T(8,128)(2,1)S(1)} collective-permute-done((bf16[2,512,128]{2,1,0:T(8,128)(2,1)S(1)}, bf16[2,512,128]{2,1,0:T(8,128)(2,1)S(1)}, u32[]{:S(2)}, u32[]{:S(2)}) %collective-permute-start.4) | collective-permute-done | bytes 262176 | tf_op jit(solution)/shard_map/ppermute | solution.py:230
  46.0 4.5 %collective-permute-done.rest_1_ = bf16[2,512,128]{2,1,0:T(8,128)(2,1)S(1)} collective-permute-done((bf16[2,512,128]{2,1,0:T(8,128)(2,1)S(1)}, bf16[2,512,128]{2,1,0:T(8,128)(2,1)S(1)}, u32[]{:S(2)}, u32[]{:S(2)}) %collective-permute-start) | collective-permute-done | bytes 262176 | tf_op jit(solution)/shard_map/ppermute | solution.py:230
  50.5 1.5 %collective-permute-start.21 = (bf16[2,512,128]{2,1,0:T(8,128)(2,1)S(1)}, bf16[2,512,128]{2,1,0:T(8,128)(2,1)S(1)}, u32[]{:S(2)}, u32[]{:S(2)}) collective-permute-start(bf16[2,512,128]{2,1,0:T(8,128)(2,1)S(1)} %get-tuple-element.22), channel_id=1, source_target_pairs={{0,2},{1,3},{2,0},{3,1},{4,6},{5,7},{6,4},{7,5},{8,10},{9,11},{10,... | collective-permute-start | bytes 786440 | tf_op jit(solution)/shard_map/ppermute | solution.py:230
  52.9 1.6 %collective-permute-start.13 = (bf16[2,512,128]{2,1,0:T(8,128)(2,1)S(1)}, bf16[2,512,128]{2,1,0:T(8,128)(2,1)S(1)}, u32[]{:S(2)}, u32[]{:S(2)}) collective-permute-start(bf16[2,512,128]{2,1,0:T(8,128)(2,1)S(1)} %get-tuple-element.26), channel_id=1, source_target_pairs={{0,2},{1,3},{2,0},{3,1},{4,6},{5,7},{6,4},{7,5},{8,10},{9,11},{10,... | collective-permute-start | bytes 786440 | tf_op jit(solution)/shard_map/ppermute | solution.py:230
  54.5 5.2 %collective-permute-done.21.rest_2_ = bf16[2,512,128]{2,1,0:T(8,128)(2,1)S(1)} collective-permute-done((bf16[2,512,128]{2,1,0:T(8,128)(2,1)S(1)}, bf16[2,512,128]{2,1,0:T(8,128)(2,1)S(1)}, u32[]{:S(2)}, u32[]{:S(2)}) %collective-permute-start.21) | collective-permute-done | bytes 262176 | tf_op jit(solution)/shard_map/ppermute | solution.py:230
  59.7 1.5 %collective-permute-start.9 = (bf16[2,512,128]{2,1,0:T(8,128)(2,1)S(1)}, bf16[2,512,128]{2,1,0:T(8,128)(2,1)S(1)}, u32[]{:S(2)}, u32[]{:S(2)}) collective-permute-start(bf16[2,512,128]{2,1,0:T(8,128)(2,1)S(1)} %get-tuple-element.28), channel_id=1, source_target_pairs={{0,2},{1,3},{2,0},{3,1},{4,6},{5,7},{6,4},{7,5},{8,10},{9,11},{10,... | collective-permute-start | bytes 786440 | tf_op jit(solution)/shard_map/ppermute | solution.py:230
  61.2 4.0 %collective-permute-done.17.rest_2_ = bf16[2,512,128]{2,1,0:T(8,128)(2,1)S(1)} collective-permute-done((bf16[2,512,128]{2,1,0:T(8,128)(2,1)S(1)}, bf16[2,512,128]{2,1,0:T(8,128)(2,1)S(1)}, u32[]{:S(2)}, u32[]{:S(2)}) %collective-permute-start.17) | collective-permute-done | bytes 262176 | tf_op jit(solution)/shard_map/ppermute | solution.py:230
  65.3 1.5 %collective-permute-start.5 = (bf16[2,512,128]{2,1,0:T(8,128)(2,1)S(1)}, bf16[2,512,128]{2,1,0:T(8,128)(2,1)S(1)}, u32[]{:S(2)}, u32[]{:S(2)}) collective-permute-start(bf16[2,512,128]{2,1,0:T(8,128)(2,1)S(1)} %get-tuple-element.30), channel_id=1, source_target_pairs={{0,2},{1,3},{2,0},{3,1},{4,6},{5,7},{6,4},{7,5},{8,10},{9,11},{10,... | collective-permute-start | bytes 786440 | tf_op jit(solution)/shard_map/ppermute | solution.py:230
  66.8 4.1 %collective-permute-done.13.rest_2_ = bf16[2,512,128]{2,1,0:T(8,128)(2,1)S(1)} collective-permute-done((bf16[2,512,128]{2,1,0:T(8,128)(2,1)S(1)}, bf16[2,512,128]{2,1,0:T(8,128)(2,1)S(1)}, u32[]{:S(2)}, u32[]{:S(2)}) %collective-permute-start.13) | collective-permute-done | bytes 262176 | tf_op jit(solution)/shard_map/ppermute | solution.py:230
  70.9 1.5 %collective-permute-start.1 = (bf16[2,512,128]{2,1,0:T(8,128)(2,1)S(1)}, bf16[2,512,128]{2,1,0:T(8,128)(2,1)S(1)}, u32[]{:S(2)}, u32[]{:S(2)}) collective-permute-start(bf16[2,512,128]{2,1,0:T(8,128)(2,1)S(1)} %get-tuple-element.32), channel_id=1, source_target_pairs={{0,2},{1,3},{2,0},{3,1},{4,6},{5,7},{6,4},{7,5},{8,10},{9,11},{10,... | collective-permute-start | bytes 786440 | tf_op jit(solution)/shard_map/ppermute | solution.py:230
  72.4 4.1 %collective-permute-done.9.rest_2_ = bf16[2,512,128]{2,1,0:T(8,128)(2,1)S(1)} collective-permute-done((bf16[2,512,128]{2,1,0:T(8,128)(2,1)S(1)}, bf16[2,512,128]{2,1,0:T(8,128)(2,1)S(1)}, u32[]{:S(2)}, u32[]{:S(2)}) %collective-permute-start.9) | collective-permute-done | bytes 262176 | tf_op jit(solution)/shard_map/ppermute | solution.py:230
  76.5 5.6 %collective-permute-done.5.rest_2_ = bf16[2,512,128]{2,1,0:T(8,128)(2,1)S(1)} collective-permute-done((bf16[2,512,128]{2,1,0:T(8,128)(2,1)S(1)}, bf16[2,512,128]{2,1,0:T(8,128)(2,1)S(1)}, u32[]{:S(2)}, u32[]{:S(2)}) %collective-permute-start.5) | collective-permute-done | bytes 262176 | tf_op jit(solution)/shard_map/ppermute | solution.py:230
  82.7 3.1 %collective-permute-done.1.rest_0_ = bf16[2,512,128]{2,1,0:T(8,128)(2,1)S(1)} collective-permute-done((bf16[2,512,128]{2,1,0:T(8,128)(2,1)S(1)}, bf16[2,512,128]{2,1,0:T(8,128)(2,1)S(1)}, u32[]{:S(2)}, u32[]{:S(2)}) %collective-permute-start.1) | collective-permute-done | bytes 262176 | tf_op jit(solution)/shard_map/ppermute | solution.py:230
  85.8 1.7 %shard_map.38 = (f32[4,144,256]{2,1,0:T(8,128)S(1)}, f32[4,8,256]{2,1,0:T(8,128)S(1)}) custom-call(bf16[256,4096]{1,0:T(8,128)(2,1)S(1)} %copy-done, bf16[2,512,128]{2,1,0:T(8,128)(2,1)S(1)} %shard_map.37.rest_0_, bf16[2,512,128]{2,1,0:T(8,128)(2,1)S(1)} %collective-permute-done.rest_1_, bf16[2,512,128]{2,1,0:T(8,128)(2,1)S(1)} %collective-permute-done.3.rest_2_), custom_call_target="tpu_custom_call" | custom-call | flops 402653184 | bytes 1310720 | tf_op jit(solution)/shard_map/pallas_call | solution.py:185
  88.2 3.3 %shard_map.46.rest_5_ = bf16[256,4096]{1,0:T(8,128)(2,1)} custom-call(bf16[256,4096]{1,0:T(8,128)(2,1)S(1)} %copy-done, bf16[2,512,128]{2,1,0:T(8,128)(2,1)S(1)} %shard_map.45.rest_0_, bf16[2,512,128]{2,1,0:T(8,128)(2,1)S(1)} %collective-permute-done.28.rest_1_, bf16[2,512,128]{2,1,0:T(8,128)(2,1)S(1)} %collective-permute-done.29.rest_2_, ...), custom_call_target="tpu_custom_call" | custom-call | flops 671088640 | bytes 1835008 | tf_op jit(solution)/shard_map/pallas_call | solution.py:185
  91.9 3.1 %shard_map.47.rest_5_ = bf16[256,4096]{1,0:T(8,128)(2,1)} custom-call(bf16[256,4096]{1,0:T(8,128)(2,1)S(1)} %copy-done, bf16[2,512,128]{2,1,0:T(8,128)(2,1)S(1)} %shard_map.44.rest_0_, bf16[2,512,128]{2,1,0:T(8,128)(2,1)S(1)} %collective-permute-done.24.rest_1_, ...), custom_call_target="tpu_custom_call", output_to_operand_aliasing={{}: (6, {})} | custom-call | flops 671088640 | bytes 1835008 | tf_op jit(solution)/shard_map/pallas_call | solution.py:185
  95.5 3.1 %shard_map.48.rest_5_ = bf16[256,4096]{1,0:T(8,128)(2,1)} custom-call(bf16[256,4096]{1,0:T(8,128)(2,1)S(1)} %copy-done, bf16[2,512,128]{2,1,0:T(8,128)(2,1)S(1)} %shard_map.43.rest_0_, bf16[2,512,128]{2,1,0:T(8,128)(2,1)S(1)} %collective-permute-done.20.rest_1_, ...), custom_call_target="tpu_custom_call", output_to_operand_aliasing={{}: (6, {})} | custom-call | flops 671088640 | bytes 1835008 | tf_op jit(solution)/shard_map/pallas_call | solution.py:185
  98.6 3.1 %shard_map.49.rest_5_ = bf16[256,4096]{1,0:T(8,128)(2,1)} custom-call(bf16[256,4096]{1,0:T(8,128)(2,1)S(1)} %copy-done, bf16[2,512,128]{2,1,0:T(8,128)(2,1)S(1)} %shard_map.42.rest_0_, bf16[2,512,128]{2,1,0:T(8,128)(2,1)S(1)} %collective-permute-done.16.rest_1_, ...), custom_call_target="tpu_custom_call", output_to_operand_aliasing={{}: (6, {})} | custom-call | flops 671088640 | bytes 1835008 | tf_op jit(solution)/shard_map/pallas_call | solution.py:185
  101.7 3.1 %shard_map.50.rest_5_ = bf16[256,4096]{1,0:T(8,128)(2,1)} custom-call(bf16[256,4096]{1,0:T(8,128)(2,1)S(1)} %copy-done, bf16[2,512,128]{2,1,0:T(8,128)(2,1)S(1)} %shard_map.41.rest_0_, bf16[2,512,128]{2,1,0:T(8,128)(2,1)S(1)} %collective-permute-done.12.rest_1_, ...), custom_call_target="tpu_custom_call", output_to_operand_aliasing={{}: (6, {})} | custom-call | flops 671088640 | bytes 1835008 | tf_op jit(solution)/shard_map/pallas_call | solution.py:185
  104.7 3.1 %shard_map.51.rest_5_ = bf16[256,4096]{1,0:T(8,128)(2,1)} custom-call(bf16[256,4096]{1,0:T(8,128)(2,1)S(1)} %copy-done, bf16[2,512,128]{2,1,0:T(8,128)(2,1)S(1)} %shard_map.40.rest_0_, bf16[2,512,128]{2,1,0:T(8,128)(2,1)S(1)} %collective-permute-done.8.rest_1_, ...), custom_call_target="tpu_custom_call", output_to_operand_aliasing={{}: (6, {})} | custom-call | flops 671088640 | bytes 1835008 | tf_op jit(solution)/shard_map/pallas_call | solution.py:185
  107.8 3.1 %shard_map.52.rest_4_ = bf16[256,4096]{1,0:T(8,128)(2,1)} custom-call(bf16[256,4096]{1,0:T(8,128)(2,1)S(1)} %copy-done, bf16[2,512,128]{2,1,0:T(8,128)(2,1)S(1)} %shard_map.39.rest_0_, bf16[2,512,128]{2,1,0:T(8,128)(2,1)S(1)} %collective-permute-done.4.rest_1_, ...), custom_call_target="tpu_custom_call", output_to_operand_aliasing={{}: (6, {})} | custom-call | flops 671088640 | bytes 1835008 | tf_op jit(solution)/shard_map/pallas_call | solution.py:185
  110.9 2.2 %shard_map.53 = bf16[256,4096]{1,0:T(8,128)(2,1)} custom-call(bf16[256,4096]{1,0:T(8,128)(2,1)S(1)} %copy-done, bf16[2,512,128]{2,1,0:T(8,128)(2,1)S(1)} %collective-permute-done.1.rest_0_, bf16[2,512,128]{2,1,0:T(8,128)(2,1)S(1)} %collective-permute-done.2.rest_1_, f32[4,144,256]{2,1,0:T(8,128)S(1)} %get-tuple-element.15.rest_2_, ...), custom_call_target="tpu_custom_call", output_to_operand_aliasing={{}: (5, {})} | custom-call | flops 268435456 | bytes 1048576 | tf_op jit(solution)/shard_map/pallas_call | solution.py:185
  (63 shorter events, 8.2 us)
Async XLA Ops:
  1.2 11.1 %collective-permute-start.28 = (bf16[2,512,128]{2,1,0:T(8,128)(2,1)S(1)}, bf16[2,512,128]{2,1,0:T(8,128)(2,1)S(1)}, u32[]{:S(2)}, u32[]{:S(2)}) collective-permute-start(bf16[2,512,128]{2,1,0:T(8,128)(2,1)S(1)} %shard_map.45.rest_0_), channel_id=1, source_target_pairs={{0,4},{1,5},{2,6},{3,7},{4,8},{5,9},{6,10},{7,11},{8,12},{9,13},{1... | collective-permute-start | bytes 786440 | tf_op jit(solution)/shard_map/ppermute | solution.py:230
  2.7 15.2 %collective-permute-start.24 = (bf16[2,512,128]{2,1,0:T(8,128)(2,1)S(1)}, bf16[2,512,128]{2,1,0:T(8,128)(2,1)S(1)}, u32[]{:S(2)}, u32[]{:S(2)}) collective-permute-start(bf16[2,512,128]{2,1,0:T(8,128)(2,1)S(1)} %shard_map.44.rest_0_), channel_id=1, source_target_pairs={{0,4},{1,5},{2,6},{3,7},{4,8},{5,9},{6,10},{7,11},{8,12},{9,13},{1... | collective-permute-start | bytes 786440 | tf_op jit(solution)/shard_map/ppermute | solution.py:230
  5.3 18.3 %collective-permute-start.20 = (bf16[2,512,128]{2,1,0:T(8,128)(2,1)S(1)}, bf16[2,512,128]{2,1,0:T(8,128)(2,1)S(1)}, u32[]{:S(2)}, u32[]{:S(2)}) collective-permute-start(bf16[2,512,128]{2,1,0:T(8,128)(2,1)S(1)} %shard_map.43.rest_0_), channel_id=1, source_target_pairs={{0,4},{1,5},{2,6},{3,7},{4,8},{5,9},{6,10},{7,11},{8,12},{9,13},{1... | collective-permute-start | bytes 786440 | tf_op jit(solution)/shard_map/ppermute | solution.py:230
  7.0 22.1 %collective-permute-start.16 = (bf16[2,512,128]{2,1,0:T(8,128)(2,1)S(1)}, bf16[2,512,128]{2,1,0:T(8,128)(2,1)S(1)}, u32[]{:S(2)}, u32[]{:S(2)}) collective-permute-start(bf16[2,512,128]{2,1,0:T(8,128)(2,1)S(1)} %shard_map.42.rest_0_), channel_id=1, source_target_pairs={{0,4},{1,5},{2,6},{3,7},{4,8},{5,9},{6,10},{7,11},{8,12},{9,13},{1... | collective-permute-start | bytes 786440 | tf_op jit(solution)/shard_map/ppermute | solution.py:230
  8.8 26.0 %collective-permute-start.12 = (bf16[2,512,128]{2,1,0:T(8,128)(2,1)S(1)}, bf16[2,512,128]{2,1,0:T(8,128)(2,1)S(1)}, u32[]{:S(2)}, u32[]{:S(2)}) collective-permute-start(bf16[2,512,128]{2,1,0:T(8,128)(2,1)S(1)} %shard_map.41.rest_0_), channel_id=1, source_target_pairs={{0,4},{1,5},{2,6},{3,7},{4,8},{5,9},{6,10},{7,11},{8,12},{9,13},{1... | collective-permute-start | bytes 786440 | tf_op jit(solution)/shard_map/ppermute | solution.py:230
  12.3 28.1 %collective-permute-start.8 = (bf16[2,512,128]{2,1,0:T(8,128)(2,1)S(1)}, bf16[2,512,128]{2,1,0:T(8,128)(2,1)S(1)}, u32[]{:S(2)}, u32[]{:S(2)}) collective-permute-start(bf16[2,512,128]{2,1,0:T(8,128)(2,1)S(1)} %shard_map.40.rest_0_), channel_id=1, source_target_pairs={{0,4},{1,5},{2,6},{3,7},{4,8},{5,9},{6,10},{7,11},{8,12},{9,13},{1... | collective-permute-start | bytes 786440 | tf_op jit(solution)/shard_map/ppermute | solution.py:230
  17.9 28.1 %collective-permute-start.4 = (bf16[2,512,128]{2,1,0:T(8,128)(2,1)S(1)}, bf16[2,512,128]{2,1,0:T(8,128)(2,1)S(1)}, u32[]{:S(2)}, u32[]{:S(2)}) collective-permute-start(bf16[2,512,128]{2,1,0:T(8,128)(2,1)S(1)} %shard_map.39.rest_0_), channel_id=1, source_target_pairs={{0,4},{1,5},{2,6},{3,7},{4,8},{5,9},{6,10},{7,11},{8,12},{9,13},{1... | collective-permute-start | bytes 786440 | tf_op jit(solution)/shard_map/ppermute | solution.py:230
  23.5 27.0 %collective-permute-start = (bf16[2,512,128]{2,1,0:T(8,128)(2,1)S(1)}, bf16[2,512,128]{2,1,0:T(8,128)(2,1)S(1)}, u32[]{:S(2)}, u32[]{:S(2)}) collective-permute-start(bf16[2,512,128]{2,1,0:T(8,128)(2,1)S(1)} %shard_map.37.rest_0_), channel_id=1, source_target_pairs={{0,4},{1,5},{2,6},{3,7},{4,8},{5,9},{6,10},{7,11},{8,12},{9,13},{1... | collective-permute-start | bytes 786440 | tf_op jit(solution)/shard_map/ppermute | solution.py:230
  29.2 22.9 %collective-permute-start.29 = (bf16[2,512,128]{2,1,0:T(8,128)(2,1)S(1)}, bf16[2,512,128]{2,1,0:T(8,128)(2,1)S(1)}, u32[]{:S(2)}, u32[]{:S(2)}) collective-permute-start(bf16[2,512,128]{2,1,0:T(8,128)(2,1)S(1)} %get-tuple-element.18), channel_id=1, source_target_pairs={{0,2},{1,3},{2,0},{3,1},{4,6},{5,7},{6,4},{7,5},{8,10},{9,11},{10,... | collective-permute-start | bytes 786440 | tf_op jit(solution)/shard_map/ppermute | solution.py:230
  34.8 17.3 %collective-permute-start.30 = (bf16[2,512,128]{2,1,0:T(8,128)(2,1)S(1)}, bf16[2,512,128]{2,1,0:T(8,128)(2,1)S(1)}, u32[]{:S(2)}, u32[]{:S(2)}) collective-permute-start(bf16[2,512,128]{2,1,0:T(8,128)(2,1)S(1)} %get-tuple-element.17), channel_id=1, source_target_pairs={{0,1},{1,0},{2,3},{3,2},{4,5},{5,4},{6,7},{7,6},{8,9},{9,8},{10,11... | collective-permute-start | bytes 786440 | tf_op jit(solution)/shard_map/ppermute | solution.py:230
  40.4 12.3 %collective-permute-start.25 = (bf16[2,512,128]{2,1,0:T(8,128)(2,1)S(1)}, bf16[2,512,128]{2,1,0:T(8,128)(2,1)S(1)}, u32[]{:S(2)}, u32[]{:S(2)}) collective-permute-start(bf16[2,512,128]{2,1,0:T(8,128)(2,1)S(1)} %get-tuple-element.20), channel_id=1, source_target_pairs={{0,2},{1,3},{2,0},{3,1},{4,6},{5,7},{6,4},{7,5},{8,10},{9,11},{10,... | collective-permute-start | bytes 786440 | tf_op jit(solution)/shard_map/ppermute | solution.py:230
  46.0 6.9 %collective-permute-start.26 = (bf16[2,512,128]{2,1,0:T(8,128)(2,1)S(1)}, bf16[2,512,128]{2,1,0:T(8,128)(2,1)S(1)}, u32[]{:S(2)}, u32[]{:S(2)}) collective-permute-start(bf16[2,512,128]{2,1,0:T(8,128)(2,1)S(1)} %get-tuple-element.19), channel_id=1, source_target_pairs={{0,1},{1,0},{2,3},{3,2},{4,5},{5,4},{6,7},{7,6},{8,9},{9,8},{10,11... | collective-permute-start | bytes 786440 | tf_op jit(solution)/shard_map/ppermute | solution.py:230
  50.5 9.2 %collective-permute-start.21 = (bf16[2,512,128]{2,1,0:T(8,128)(2,1)S(1)}, bf16[2,512,128]{2,1,0:T(8,128)(2,1)S(1)}, u32[]{:S(2)}, u32[]{:S(2)}) collective-permute-start(bf16[2,512,128]{2,1,0:T(8,128)(2,1)S(1)} %get-tuple-element.22), channel_id=1, source_target_pairs={{0,2},{1,3},{2,0},{3,1},{4,6},{5,7},{6,4},{7,5},{8,10},{9,11},{10,... | collective-permute-start | bytes 786440 | tf_op jit(solution)/shard_map/ppermute | solution.py:230
  52.0 7.7 %collective-permute-start.22 = (bf16[2,512,128]{2,1,0:T(8,128)(2,1)S(1)}, bf16[2,512,128]{2,1,0:T(8,128)(2,1)S(1)}, u32[]{:S(2)}, u32[]{:S(2)}) collective-permute-start(bf16[2,512,128]{2,1,0:T(8,128)(2,1)S(1)} %get-tuple-element.21), channel_id=1, source_target_pairs={{0,1},{1,0},{2,3},{3,2},{4,5},{5,4},{6,7},{7,6},{8,9},{9,8},{10,11... | collective-permute-start | bytes 786440 | tf_op jit(solution)/shard_map/ppermute | solution.py:230
  52.1 13.2 %collective-permute-start.17 = (bf16[2,512,128]{2,1,0:T(8,128)(2,1)S(1)}, bf16[2,512,128]{2,1,0:T(8,128)(2,1)S(1)}, u32[]{:S(2)}, u32[]{:S(2)}) collective-permute-start(bf16[2,512,128]{2,1,0:T(8,128)(2,1)S(1)} %get-tuple-element.24), channel_id=1, source_target_pairs={{0,2},{1,3},{2,0},{3,1},{4,6},{5,7},{6,4},{7,5},{8,10},{9,11},{10,... | collective-permute-start | bytes 786440 | tf_op jit(solution)/shard_map/ppermute | solution.py:230
  52.7 14.2 %collective-permute-start.18 = (bf16[2,512,128]{2,1,0:T(8,128)(2,1)S(1)}, bf16[2,512,128]{2,1,0:T(8,128)(2,1)S(1)}, u32[]{:S(2)}, u32[]{:S(2)}) collective-permute-start(bf16[2,512,128]{2,1,0:T(8,128)(2,1)S(1)} %get-tuple-element.23), channel_id=1, source_target_pairs={{0,1},{1,0},{2,3},{3,2},{4,5},{5,4},{6,7},{7,6},{8,9},{9,8},{10,11... | collective-permute-start | bytes 786440 | tf_op jit(solution)/shard_map/ppermute | solution.py:230
  52.9 18.0 %collective-permute-start.13 = (bf16[2,512,128]{2,1,0:T(8,128)(2,1)S(1)}, bf16[2,512,128]{2,1,0:T(8,128)(2,1)S(1)}, u32[]{:S(2)}, u32[]{:S(2)}) collective-permute-start(bf16[2,512,128]{2,1,0:T(8,128)(2,1)S(1)} %get-tuple-element.26), channel_id=1, source_target_pairs={{0,2},{1,3},{2,0},{3,1},{4,6},{5,7},{6,4},{7,5},{8,10},{9,11},{10,... | collective-permute-start | bytes 786440 | tf_op jit(solution)/shard_map/ppermute | solution.py:230
  59.7 12.8 %collective-permute-start.14 = (bf16[2,512,128]{2,1,0:T(8,128)(2,1)S(1)}, bf16[2,512,128]{2,1,0:T(8,128)(2,1)S(1)}, u32[]{:S(2)}, u32[]{:S(2)}) collective-permute-start(bf16[2,512,128]{2,1,0:T(8,128)(2,1)S(1)} %get-tuple-element.25), channel_id=1, source_target_pairs={{0,1},{1,0},{2,3},{3,2},{4,5},{5,4},{6,7},{7,6},{8,9},{9,8},{10,11... | collective-permute-start | bytes 786440 | tf_op jit(solution)/shard_map/ppermute | solution.py:230
  59.7 16.8 %collective-permute-start.9 = (bf16[2,512,128]{2,1,0:T(8,128)(2,1)S(1)}, bf16[2,512,128]{2,1,0:T(8,128)(2,1)S(1)}, u32[]{:S(2)}, u32[]{:S(2)}) collective-permute-start(bf16[2,512,128]{2,1,0:T(8,128)(2,1)S(1)} %get-tuple-element.28), channel_id=1, source_target_pairs={{0,2},{1,3},{2,0},{3,1},{4,6},{5,7},{6,4},{7,5},{8,10},{9,11},{10,... | collective-permute-start | bytes 786440 | tf_op jit(solution)/shard_map/ppermute | solution.py:230
  65.3 16.9 %collective-permute-start.5 = (bf16[2,512,128]{2,1,0:T(8,128)(2,1)S(1)}, bf16[2,512,128]{2,1,0:T(8,128)(2,1)S(1)}, u32[]{:S(2)}, u32[]{:S(2)}) collective-permute-start(bf16[2,512,128]{2,1,0:T(8,128)(2,1)S(1)} %get-tuple-element.30), channel_id=1, source_target_pairs={{0,2},{1,3},{2,0},{3,1},{4,6},{5,7},{6,4},{7,5},{8,10},{9,11},{10,... | collective-permute-start | bytes 786440 | tf_op jit(solution)/shard_map/ppermute | solution.py:230
  66.8 15.3 %collective-permute-start.3 = (bf16[2,512,128]{2,1,0:T(8,128)(2,1)S(1)}, bf16[2,512,128]{2,1,0:T(8,128)(2,1)S(1)}, u32[]{:S(2)}, u32[]{:S(2)}) collective-permute-start(bf16[2,512,128]{2,1,0:T(8,128)(2,1)S(1)} %get-tuple-element.31), channel_id=1, source_target_pairs={{0,1},{1,0},{2,3},{3,2},{4,5},{5,4},{6,7},{7,6},{8,9},{9,8},{10,11... | collective-permute-start | bytes 786440 | tf_op jit(solution)/shard_map/ppermute | solution.py:230
  70.9 14.9 %collective-permute-start.1 = (bf16[2,512,128]{2,1,0:T(8,128)(2,1)S(1)}, bf16[2,512,128]{2,1,0:T(8,128)(2,1)S(1)}, u32[]{:S(2)}, u32[]{:S(2)}) collective-permute-start(bf16[2,512,128]{2,1,0:T(8,128)(2,1)S(1)} %get-tuple-element.32), channel_id=1, source_target_pairs={{0,2},{1,3},{2,0},{3,1},{4,6},{5,7},{6,4},{7,5},{8,10},{9,11},{10,... | collective-permute-start | bytes 786440 | tf_op jit(solution)/shard_map/ppermute | solution.py:230
  72.4 15.0 %collective-permute-start.31 = (bf16[2,512,128]{2,1,0:T(8,128)(2,1)S(1)}, bf16[2,512,128]{2,1,0:T(8,128)(2,1)S(1)}, u32[]{:S(2)}, u32[]{:S(2)}) collective-permute-start(bf16[2,512,128]{2,1,0:T(8,128)(2,1)S(1)} %collective-permute-done.29.rest_2_), channel_id=1, source_target_pairs={{0,1},{1,0},{2,3},{3,2},{4,5},{5,4},{6,7},{7,6},{8,9},{9,8},{10,11... | collective-permute-start | bytes 786440 | tf_op jit(solution)/shard_map/ppermute | solution.py:230
  76.5 11.5 %collective-permute-start.27 = (bf16[2,512,128]{2,1,0:T(8,128)(2,1)S(1)}, bf16[2,512,128]{2,1,0:T(8,128)(2,1)S(1)}, u32[]{:S(2)}, u32[]{:S(2)}) collective-permute-start(bf16[2,512,128]{2,1,0:T(8,128)(2,1)S(1)} %collective-permute-done.25.rest_2_), channel_id=1, source_target_pairs={{0,1},{1,0},{2,3},{3,2},{4,5},{5,4},{6,7},{7,6},{8,9},{9,8},{10,11... | collective-permute-start | bytes 786440 | tf_op jit(solution)/shard_map/ppermute | solution.py:230
  82.1 9.3 %collective-permute-start.23 = (bf16[2,512,128]{2,1,0:T(8,128)(2,1)S(1)}, bf16[2,512,128]{2,1,0:T(8,128)(2,1)S(1)}, u32[]{:S(2)}, u32[]{:S(2)}) collective-permute-start(bf16[2,512,128]{2,1,0:T(8,128)(2,1)S(1)} %collective-permute-done.21.rest_2_), channel_id=1, source_target_pairs={{0,1},{1,0},{2,3},{3,2},{4,5},{5,4},{6,7},{7,6},{8,9},{9,8},{10,11... | collective-permute-start | bytes 786440 | tf_op jit(solution)/shard_map/ppermute | solution.py:230
  82.2 9.7 %collective-permute-start.19 = (bf16[2,512,128]{2,1,0:T(8,128)(2,1)S(1)}, bf16[2,512,128]{2,1,0:T(8,128)(2,1)S(1)}, u32[]{:S(2)}, u32[]{:S(2)}) collective-permute-start(bf16[2,512,128]{2,1,0:T(8,128)(2,1)S(1)} %collective-permute-done.17.rest_2_), channel_id=1, source_target_pairs={{0,1},{1,0},{2,3},{3,2},{4,5},{5,4},{6,7},{7,6},{8,9},{9,8},{10,11... | collective-permute-start | bytes 786440 | tf_op jit(solution)/shard_map/ppermute | solution.py:230
  85.8 9.3 %collective-permute-start.15 = (bf16[2,512,128]{2,1,0:T(8,128)(2,1)S(1)}, bf16[2,512,128]{2,1,0:T(8,128)(2,1)S(1)}, u32[]{:S(2)}, u32[]{:S(2)}) collective-permute-start(bf16[2,512,128]{2,1,0:T(8,128)(2,1)S(1)} %collective-permute-done.13.rest_2_), channel_id=1, source_target_pairs={{0,1},{1,0},{2,3},{3,2},{4,5},{5,4},{6,7},{7,6},{8,9},{9,8},{10,11... | collective-permute-start | bytes 786440 | tf_op jit(solution)/shard_map/ppermute | solution.py:230
  87.5 17.2 %collective-permute-start.10 = (bf16[2,512,128]{2,1,0:T(8,128)(2,1)S(1)}, bf16[2,512,128]{2,1,0:T(8,128)(2,1)S(1)}, u32[]{:S(2)}, u32[]{:S(2)}) collective-permute-start(bf16[2,512,128]{2,1,0:T(8,128)(2,1)S(1)} %get-tuple-element.27), channel_id=1, source_target_pairs={{0,1},{1,0},{2,3},{3,2},{4,5},{5,4},{6,7},{7,6},{8,9},{9,8},{10,11... | collective-permute-start | bytes 786440 | tf_op jit(solution)/shard_map/ppermute | solution.py:230
  88.1 16.7 %collective-permute-start.11 = (bf16[2,512,128]{2,1,0:T(8,128)(2,1)S(1)}, bf16[2,512,128]{2,1,0:T(8,128)(2,1)S(1)}, u32[]{:S(2)}, u32[]{:S(2)}) collective-permute-start(bf16[2,512,128]{2,1,0:T(8,128)(2,1)S(1)} %collective-permute-done.9.rest_2_), channel_id=1, source_target_pairs={{0,1},{1,0},{2,3},{3,2},{4,5},{5,4},{6,7},{7,6},{8,9},{9,8},{10,11... | collective-permute-start | bytes 786440 | tf_op jit(solution)/shard_map/ppermute | solution.py:230
  91.4 16.4 %collective-permute-start.6 = (bf16[2,512,128]{2,1,0:T(8,128)(2,1)S(1)}, bf16[2,512,128]{2,1,0:T(8,128)(2,1)S(1)}, u32[]{:S(2)}, u32[]{:S(2)}) collective-permute-start(bf16[2,512,128]{2,1,0:T(8,128)(2,1)S(1)} %get-tuple-element.29), channel_id=1, source_target_pairs={{0,1},{1,0},{2,3},{3,2},{4,5},{5,4},{6,7},{7,6},{8,9},{9,8},{10,11... | collective-permute-start | bytes 786440 | tf_op jit(solution)/shard_map/ppermute | solution.py:230
  91.9 16.0 %collective-permute-start.7 = (bf16[2,512,128]{2,1,0:T(8,128)(2,1)S(1)}, bf16[2,512,128]{2,1,0:T(8,128)(2,1)S(1)}, u32[]{:S(2)}, u32[]{:S(2)}) collective-permute-start(bf16[2,512,128]{2,1,0:T(8,128)(2,1)S(1)} %collective-permute-done.5.rest_2_), channel_id=1, source_target_pairs={{0,1},{1,0},{2,3},{3,2},{4,5},{5,4},{6,7},{7,6},{8,9},{9,8},{10,11... | collective-permute-start | bytes 786440 | tf_op jit(solution)/shard_map/ppermute | solution.py:230
  95.0 15.9 %collective-permute-start.2 = (bf16[2,512,128]{2,1,0:T(8,128)(2,1)S(1)}, bf16[2,512,128]{2,1,0:T(8,128)(2,1)S(1)}, u32[]{:S(2)}, u32[]{:S(2)}) collective-permute-start(bf16[2,512,128]{2,1,0:T(8,128)(2,1)S(1)} %collective-permute-done.1.rest_0_), channel_id=1, source_target_pairs={{0,1},{1,0},{2,3},{3,2},{4,5},{5,4},{6,7},{7,6},{8,9},{9,8},{10,11... | collective-permute-start | bytes 786440 | tf_op jit(solution)/shard_map/ppermute | solution.py:230
  (3 other events, 50.5 us)
